TPU v7x, 32 devices: a whole 2x2x4 slice. The times are simulated.
32 devices in a mesh: dp: 16 (over z, y, x), tensor: 2 (over core).
Axes of the slice: x: 2, y: 2, z: 4, core: 2. Of those that a mesh axis runs over, the one named last changes fastest.
Arguments:
- tokens: bfloat16 [24576, 768], P(('dp', 'tensor')), may hold values from -6 to 6
- kept_patches: int32 [24576], P(('dp', 'tensor')), may hold values from 0 to 1567, as said below
- clip_lengths: int32 [128], replicated, may hold values from 39 to 314, as said below
- clip_device: int32 [128], replicated, may hold values from 0 to 31, as said below
- cot_output: bfloat16 [24576, 768], P(('dp', 'tensor')), may hold values from -6 to 6
- cot_aligned: bfloat16 [24576, 1024], P(('dp', 'tensor')), may hold values from -6 to 6
- entry_weight: float32 [1769472], P(('dp', 'tensor')), may hold values from -0.21875 to 0.21875
- entry_first: float32 [1769472], P(('dp', 'tensor')), may hold values from -112 to 112
- entry_second: float32 [1769472], P(('dp', 'tensor')), may hold values from 245.76 to 4096.8193
- exit_weight: float32 [589824], P(('dp', 'tensor')), may hold values from -1.75 to 1.75
- exit_first: float32 [589824], P(('dp', 'tensor')), may hold values from -24 to 24
- exit_second: float32 [589824], P(('dp', 'tensor')), may hold values from 12.288 to 204.71808
- align_weight: float32 [786432], P(('dp', 'tensor')), may hold values from -0.21875 to 0.21875
- align_first: float32 [786432], P(('dp', 'tensor')), may hold values from -128 to 128
- align_second: float32 [786432], P(('dp', 'tensor')), may hold values from 447.2832 to 8183.808
- expand_weight: float32 [3072, 768], P(('dp', 'tensor')), may hold values from -0.21875 to 0.21875
- expand_first: float32 [3072, 768], P(('dp', 'tensor')), may hold values from -32 to 32
- expand_second: float32 [3072, 768], P(('dp', 'tensor')), may hold values from 24.576 to 409.68192
- reduce_weight: float32 [3072, 768], P(('dp', 'tensor')), may hold values from -0.109375 to 0.109375
- reduce_first: float32 [3072, 768], P(('dp', 'tensor')), may hold values from -80 to 80
- reduce_second: float32 [3072, 768], P(('dp', 'tensor')), may hold values from 144.50688 to 2457.6
- position_table: float32 [1204224], P(('dp', 'tensor')), may hold values from -3 to 3
- position_first: float32 [1204224], P(('dp', 'tensor')), may hold values from -5 to 5
- position_second: float32 [1204224], P(('dp', 'tensor')), may hold values from 0.5219265 to 7.836735
- norm_params: float32 [3072], P(('dp', 'tensor')), may hold values from -1.5 to 1.5, as said below
- norm_first: float32 [3072], P(('dp', 'tensor')), may hold values from -128 to 128
- norm_second: float32 [3072], P(('dp', 'tensor')), may hold values from 447.2832 to 8183.808
Outputs:
- block_out: bfloat16 [24576, 768], P(('dp', 'tensor'))
- aligned: bfloat16 [24576, 1024], P(('dp', 'tensor'))
- token_grad: float32 [24576, 768], P(('dp', 'tensor'))
- new_entry_first: float32 [1769472], P(('dp', 'tensor'))
- new_entry_second: float32 [1769472], P(('dp', 'tensor'))
- new_entry_weight: float32 [1769472], P(('dp', 'tensor'))
- new_exit_first: float32 [589824], P(('dp', 'tensor'))
- new_exit_second: float32 [589824], P(('dp', 'tensor'))
- new_exit_weight: float32 [589824], P(('dp', 'tensor'))
- new_align_first: float32 [786432], P(('dp', 'tensor'))
- new_align_second: float32 [786432], P(('dp', 'tensor'))
- new_align_weight: float32 [786432], P(('dp', 'tensor'))
- new_expand_first: float32 [3072, 768], P(('dp', 'tensor'))
- new_expand_second: float32 [3072, 768], P(('dp', 'tensor'))
- new_expand_weight: float32 [3072, 768], P(('dp', 'tensor'))
- new_reduce_first: float32 [3072, 768], P(('dp', 'tensor'))
- new_reduce_second: float32 [3072, 768], P(('dp', 'tensor'))
- new_reduce_weight: float32 [3072, 768], P(('dp', 'tensor'))
- new_position_first: float32 [1204224], P(('dp', 'tensor'))
- new_position_second: float32 [1204224], P(('dp', 'tensor'))
- new_position_table: float32 [1204224], P(('dp', 'tensor'))
- new_norm_first: float32 [3072], P(('dp', 'tensor'))
- new_norm_second: float32 [3072], P(('dp', 'tensor'))
- new_norm_params: float32 [3072], P(('dp', 'tensor'))
- lamb_stats: float32 [3, 7], replicated
Inputs may be any that keep to these rules, and one draw needn't show every extreme that they name: `clip_lengths`: every clip has 314 rows (a video clip) or 39 rows (an image). `clip_device`: each device index d = i * 2 + j holds exactly 4 clips, at most 2 of them video clips, and some device holds 2. `kept_patches`: within a video clip the rows hold distinct positions below 1568 in rising order, within an image distinct positions below 196 in rising order; padding rows hold 0. `norm_params`: gains lie in 0.5 to 1.5; shifts are normal of deviation 0.5, held within -1.5 to 1.5.
All inputs are finite; a program needn't handle non-finite values.
Results may differ from a plain program's by a relative error of at most 0.0085.
The roundings to bfloat16 on the way count: a program that leaves them out, or rounds other values in their place, can miss the bound.
Values may be sent and summed in bfloat16 or wider, within the bound.
A program may use at most 192 MiB of HBM per device.

v0:
```python
import jax
import jax.numpy as jnp
from jax import lax
from jax.sharding import PartitionSpec as P

H = 12
HD = 64
LN_EPS = 1e-06
MASKED = -1e30
RATE = 0.5
BETA_ONE = 0.9
BETA_TWO = 0.98
ADAM_EPS = 1e-06
DECAY = 0.05
TINY = 1e-06


def contract(left, right, left_dim, right_dim):
    return lax.dot_general(
        left, right, (((left_dim,), (right_dim,)), ((), ())), preferred_element_type=jnp.float32
    )


def layer_norm(values, gain, shift):
    center = values - jnp.mean(values, axis=-1, keepdims=True)
    spread = jnp.mean(center * center, axis=-1, keepdims=True)
    return center * lax.rsqrt(spread + LN_EPS) * gain + shift


def gelu_exact(values):
    return jax.nn.gelu(values, approximate=False)


def row_layout(clip_lengths, clip_device, device, row_count):
    mine = clip_device == device
    own_length = jnp.where(mine, clip_lengths, 0)
    starts = jnp.cumsum(own_length) - own_length
    filled = jnp.sum(own_length)
    positions = jnp.arange(row_count, dtype=jnp.int32)
    begun = mine[None, :] & (starts[None, :] <= positions[:, None])
    segment = jnp.sum(begun.astype(jnp.int32), axis=1)
    valid_rows = positions < filled
    return (jnp.where(valid_rows, segment, 0), valid_rows)


def head_scores(queries, key_rows, same_clip, score_scale):
    scores = contract(queries, key_rows, 1, 1) * score_scale
    return jnp.where(same_clip, scores, MASKED)


def head_forward(queries, key_rows, value_rows, same_clip, score_scale):
    scores = head_scores(queries, key_rows, same_clip, score_scale)
    peak_score = jnp.max(scores, axis=1, keepdims=True)
    raised = jnp.exp(scores - peak_score)
    row_total = jnp.sum(raised, axis=1, keepdims=True)
    attention = raised / row_total
    result = jnp.dot(attention.astype(jnp.bfloat16), value_rows, preferred_element_type=jnp.float32)
    return (result, (peak_score + jnp.log(row_total))[:, 0])


def head_backward(queries, key_rows, value_rows, log_total, grad_heads, same_clip, score_scale):
    scores = head_scores(queries, key_rows, same_clip, score_scale)
    attention = jnp.exp(scores - log_total[:, None])
    attention_low = attention.astype(jnp.bfloat16)
    grad_values = contract(attention_low, grad_heads, 0, 0)
    grad_attention = contract(grad_heads, value_rows, 1, 1)
    inner = jnp.sum(attention * grad_attention, axis=1, keepdims=True)
    grad_score = (attention * (grad_attention - inner)).astype(jnp.bfloat16)
    grad_queries = jnp.dot(grad_score, key_rows, preferred_element_type=jnp.float32) * score_scale
    grad_keys = contract(grad_score, queries, 0, 0) * score_scale
    return (grad_queries, grad_keys, grad_values)


def lamb_moments(weight, gradient, first, second, decay):
    new_first = BETA_ONE * first + (1.0 - BETA_ONE) * gradient
    new_second = BETA_TWO * second + (1.0 - BETA_TWO) * gradient * gradient
    update = new_first / (jnp.sqrt(new_second) + ADAM_EPS) + decay * weight
    return (new_first, new_second, update)


def local(
    tokens,
    kept_patches,
    clip_lengths,
    clip_device,
    cot_output,
    cot_aligned,
    entry_weight,
    entry_first,
    entry_second,
    exit_weight,
    exit_first,
    exit_second,
    align_weight,
    align_first,
    align_second,
    expand_weight,
    expand_first,
    expand_second,
    reduce_weight,
    reduce_first,
    reduce_second,
    position_table,
    position_first,
    position_second,
    norm_params,
    norm_first,
    norm_second,
):
    row_count, model_width = tokens.shape
    align_width = cot_aligned.shape[1]
    score_scale = HD ** (-0.5)
    masters = (
        entry_weight,
        exit_weight,
        align_weight,
        expand_weight,
        reduce_weight,
        position_table,
        norm_params,
    )
    device = lax.axis_index("dp") * lax.axis_size("tensor") + lax.axis_index("tensor")
    segment, valid_rows = row_layout(clip_lengths, clip_device, device, row_count)
    same_clip = segment[:, None] == segment[None, :]
    valid_column = valid_rows[:, None]
    gathered = (
        lax.all_gather(entry_weight.astype(jnp.bfloat16), ("dp", "tensor"), axis=0, tiled=True),
        lax.all_gather(exit_weight.astype(jnp.bfloat16), ("dp", "tensor"), axis=0, tiled=True),
        lax.all_gather(align_weight.astype(jnp.bfloat16), ("dp", "tensor"), axis=0, tiled=True),
        lax.all_gather(position_table.astype(jnp.bfloat16), ("dp", "tensor"), axis=0, tiled=True),
        lax.all_gather(norm_params.astype(jnp.bfloat16), ("dp", "tensor"), axis=0, tiled=True),
    )
    expand_low, reduce_low = (
        lax.all_gather(expand_weight.astype(jnp.bfloat16), "dp", axis=0, tiled=True),
        lax.all_gather(reduce_weight.astype(jnp.bfloat16), "dp", axis=0, tiled=True),
    )
    entry_low = gathered[0].reshape(model_width, 3 * model_width)
    exit_low = gathered[1].reshape(model_width, model_width)
    align_low = gathered[2].reshape(model_width, align_width)
    table_low = gathered[3].reshape(-1, model_width)
    norm_low = gathered[4].astype(jnp.float32).reshape(4, model_width)
    residual = tokens.astype(jnp.float32) + jnp.take(table_low, kept_patches, axis=0).astype(
        jnp.float32
    )
    normed_one = layer_norm(residual, norm_low[0], norm_low[1]).astype(jnp.bfloat16)
    joint_low = jnp.dot(normed_one, entry_low, preferred_element_type=jnp.float32).astype(
        jnp.bfloat16
    )
    split_heads = joint_low.reshape(row_count, 3, H, HD).transpose(1, 2, 0, 3)
    head_outputs, log_totals = lax.map(
        lambda entries: head_forward(entries[0], entries[1], entries[2], same_clip, score_scale),
        (split_heads[0], split_heads[1], split_heads[2]),
    )
    attended = head_outputs.transpose(1, 0, 2).reshape(row_count, model_width).astype(jnp.bfloat16)
    middle = residual + jnp.dot(attended, exit_low, preferred_element_type=jnp.float32)
    normed_two = layer_norm(middle, norm_low[2], norm_low[3]).astype(jnp.bfloat16)
    hidden_in = lax.all_gather(normed_two, "tensor", axis=0, tiled=True)
    hidden_pre = contract(hidden_in, expand_low, 1, 1)
    hidden_act = gelu_exact(hidden_pre).astype(jnp.bfloat16)
    feed_out = lax.psum_scatter(
        jnp.dot(hidden_act, reduce_low, preferred_element_type=jnp.float32).astype(jnp.bfloat16),
        "tensor",
        scatter_dimension=0,
        tiled=True,
    ).astype(jnp.float32)
    out_low = (middle + feed_out).astype(jnp.bfloat16)
    block_out = jnp.where(valid_column, out_low, jnp.zeros_like(out_low))
    align_rows = jnp.dot(out_low, align_low, preferred_element_type=jnp.float32).astype(
        jnp.bfloat16
    )
    aligned = jnp.where(valid_column, align_rows, jnp.zeros_like(align_rows))
    cot_align_valid = jnp.where(valid_column, cot_aligned, jnp.zeros_like(cot_aligned))
    grad_align = contract(out_low, cot_align_valid, 0, 0)
    grad_out = jnp.where(valid_column, cot_output.astype(jnp.float32), 0.0) + contract(
        cot_align_valid, align_low, 1, 1
    )
    grad_feed = grad_out.astype(jnp.bfloat16)
    grad_feed_rows = lax.all_gather(grad_feed, "tensor", axis=0, tiled=True)
    grad_act = contract(grad_feed_rows, reduce_low, 1, 1)
    gelu_value, gelu_back = jax.vjp(gelu_exact, hidden_pre)
    grad_pre = gelu_back(grad_act)[0].astype(jnp.bfloat16)
    grad_reduce = contract(hidden_act, grad_feed_rows, 0, 0)
    grad_expand = contract(grad_pre, hidden_in, 0, 0)
    grad_two = lax.psum_scatter(
        jnp.dot(grad_pre, expand_low, preferred_element_type=jnp.float32),
        "tensor",
        scatter_dimension=0,
        tiled=True,
    )
    grad_expand, grad_reduce = (
        lax.psum_scatter(grad_expand, "dp", scatter_dimension=0, tiled=True),
        lax.psum_scatter(grad_reduce, "dp", scatter_dimension=0, tiled=True),
    )
    norm_value, norm_back_two = jax.vjp(layer_norm, middle, norm_low[2], norm_low[3])
    grad_from_two, grad_gain_two, grad_shift_two = norm_back_two(grad_two)
    grad_middle = grad_out + grad_from_two
    grad_branch = grad_middle.astype(jnp.bfloat16)
    grad_exit = contract(attended, grad_branch, 0, 0)
    grad_attended = contract(grad_branch, exit_low, 1, 1).astype(jnp.bfloat16)
    grad_heads = grad_attended.reshape(row_count, H, HD).transpose(1, 0, 2)
    grad_queries, grad_keys, grad_values = lax.map(
        lambda entries: head_backward(
            entries[0], entries[1], entries[2], entries[3], entries[4], same_clip, score_scale
        ),
        (split_heads[0], split_heads[1], split_heads[2], log_totals, grad_heads),
    )
    grad_joint = jnp.stack((grad_queries, grad_keys, grad_values)).transpose(2, 0, 1, 3)
    grad_joint = grad_joint.reshape(row_count, 3 * model_width).astype(jnp.bfloat16)
    grad_entry = contract(normed_one, grad_joint, 0, 0)
    grad_one = contract(grad_joint, entry_low, 1, 1)
    norm_value_one, norm_back_one = jax.vjp(layer_norm, residual, norm_low[0], norm_low[1])
    grad_from_one, grad_gain_one, grad_shift_one = norm_back_one(grad_one)
    token_grad = grad_middle + grad_from_one
    grad_table = jax.ops.segment_sum(token_grad, kept_patches, num_segments=table_low.shape[0])
    grad_norms = jnp.concatenate((grad_gain_one, grad_shift_one, grad_gain_two, grad_shift_two))
    summed = (
        lax.psum_scatter(grad_entry.reshape(-1), ("dp", "tensor"), scatter_dimension=0, tiled=True),
        lax.psum_scatter(grad_exit.reshape(-1), ("dp", "tensor"), scatter_dimension=0, tiled=True),
        lax.psum_scatter(grad_align.reshape(-1), ("dp", "tensor"), scatter_dimension=0, tiled=True),
        lax.psum_scatter(grad_table.reshape(-1), ("dp", "tensor"), scatter_dimension=0, tiled=True),
        lax.psum_scatter(grad_norms, ("dp", "tensor"), scatter_dimension=0, tiled=True),
    )
    gradients = (summed[0], summed[1], summed[2], grad_expand, grad_reduce, summed[3], summed[4])
    firsts = (
        entry_first,
        exit_first,
        align_first,
        expand_first,
        reduce_first,
        position_first,
        norm_first,
    )
    seconds = (
        entry_second,
        exit_second,
        align_second,
        expand_second,
        reduce_second,
        position_second,
        norm_second,
    )
    decays = (DECAY, DECAY, DECAY, DECAY, DECAY, DECAY, 0.0)
    results = [
        lamb_moments(
            masters[member], gradients[member], firsts[member], seconds[member], decays[member]
        )
        for member in range(7)
    ]
    update_local = jnp.stack([jnp.sum(found[2] * found[2]) for found in results])
    weight_squares, update_squares = lax.psum(
        (jnp.stack([jnp.sum(master * master) for master in masters]), update_local),
        ("dp", "tensor"),
    )
    trust = jnp.sqrt(weight_squares) / jnp.sqrt(update_squares + TINY)
    outputs = [block_out, aligned, token_grad]
    for member in range(7):
        found = results[member]
        outputs = outputs + [found[0], found[1], masters[member] - RATE * trust[member] * found[2]]
    lamb_stats = jnp.stack((trust, jnp.sqrt(weight_squares), jnp.sqrt(update_squares)))
    outputs = outputs + [lamb_stats]
    return tuple(outputs)


def solution(mesh):
    placed = (
        P(("dp", "tensor"), None),
        P(("dp", "tensor")),
        P(),
        P(),
        P(("dp", "tensor"), None),
        P(("dp", "tensor"), None),
        P(("dp", "tensor")),
        P(("dp", "tensor")),
        P(("dp", "tensor")),
        P(("dp", "tensor")),
        P(("dp", "tensor")),
        P(("dp", "tensor")),
        P(("dp", "tensor")),
        P(("dp", "tensor")),
        P(("dp", "tensor")),
        P(("dp", "tensor"), None),
        P(("dp", "tensor"), None),
        P(("dp", "tensor"), None),
        P(("dp", "tensor"), None),
        P(("dp", "tensor"), None),
        P(("dp", "tensor"), None),
        P(("dp", "tensor")),
        P(("dp", "tensor")),
        P(("dp", "tensor")),
        P(("dp", "tensor")),
        P(("dp", "tensor")),
        P(("dp", "tensor")),
    )
    return jax.shard_map(
        local,
        mesh=mesh,
        in_specs=placed,
        out_specs=(
            P(("dp", "tensor"), None),
            P(("dp", "tensor"), None),
            P(("dp", "tensor"), None),
            P(("dp", "tensor")),
            P(("dp", "tensor")),
            P(("dp", "tensor")),
            P(("dp", "tensor")),
            P(("dp", "tensor")),
            P(("dp", "tensor")),
            P(("dp", "tensor")),
            P(("dp", "tensor")),
            P(("dp", "tensor")),
            P(("dp", "tensor"), None),
            P(("dp", "tensor"), None),
            P(("dp", "tensor"), None),
            P(("dp", "tensor"), None),
            P(("dp", "tensor"), None),
            P(("dp", "tensor"), None),
            P(("dp", "tensor")),
            P(("dp", "tensor")),
            P(("dp", "tensor")),
            P(("dp", "tensor")),
            P(("dp", "tensor")),
            P(("dp", "tensor")),
            P(),
        ),
        check_vma=False,
    )
```

profile of v0, /device:TPU:0, one launch (start us, length us, event | category | flops | bytes accessed | tf_op | source)
XLA Modules:
  0.0 1165.3 jit_solution(5532540820435427545)
XLA Ops:
  19.3 42.3 %all-reduce = bf16[3072]{0:T(1024)(128)(2,1)S(1)} all-reduce(bf16[3072]{0:T(1024)(128)(2,1)S(1)} %dynamic-update-slice), channel_id=1, replica_groups=mesh['dp'=16,'tensor'=2] {'dp','tensor'}, use_global_device_ids=true, to_apply=%add | all-reduce | flops 3072 | bytes 12288
  64.1 4.3 all-gather.12.cloned.1.call-done
  68.4 3.3 reshape.249
  71.7 63.2 %all-gather.24.cloned.1.call-done = bf16[32,1,37632]{2,1,0:T(2,128)(2,1)} async-done(((bf16[1,1,37632]{2,1,0:T(2,128)(2,1)}), bf16[32,1,37632]{2,1,0:T(2,128)(2,1)}) %all-gather.24.cloned.1.call-update) | async-done | bytes 2408464 | tf_op jit(solution)/shard_map/all_gather | solution.py:130
  135.0 51.2 %reduce.1 = bf16[32,37632]{1,0:T(8,128)(2,1)} reduce(bf16[32,1,37632]{2,1,0:T(2,128)(2,1)} %all-gather.24.cloned.1.call-done, bf16[]{:T(256)} %constant.226), dimensions={1}, to_apply=%all-gather.reduce_sub_computation | reduce | bytes 4816898 | tf_op jit(solution)/shard_map/all_gather | solution.py:130
  186.1 5.0 reshape.244
  191.1 3.4 gather_fusion
  197.4 7.6 reshape.245
  205.0 7.2 convolution_convert_fusion
  212.2 5.8 copy.127
  217.9 3.3 slice_bitcast_fusion
  221.2 3.7 copy.129
  227.3 2.5 copy.131
  230.9 64.8 %while.28 = (s32[]{:T(128)}, bf16[12,768,64]{1,2,0:T(8,128)(2,1)}, f32[12,768]{1,0:T(8,128)}, bf16[12,768,64]{2,1,0:T(8,128)(2,1)}, bf16[12,768,64]{2,1,0:T(8,12...) while((s32[]{:T(128)}, bf16[12,768,64]{1,2,0:T(8,128)(2,1)}, ...), condition=%wide.region_8.9_spmd.clone, body=%wide.region_5.8_spmd.clone.sunk | while | flops 156302592 | bytes 7911521 | solution.py:150
  295.7 3.2 fusion.89
  304.5 3.7 reshape.250
  308.2 5.2 fusion.90
  313.5 5.4 all-gather.16.cloned.1.call-done
  318.9 11.2 all-gather.14.cloned.1.call-done
  330.1 27.0 %multiply_convert_fusion.1 = (bf16[1536,1536]{1,0:T(8,128)(2,1)}, f32[1536,1536]{1,0:T(8,128)}, f32[1536,1536]{1,0:T(8,128)}) fusion(bf16[1536,768]{0,1:T(8,128)(2,1)} %all-gather.14.cloned.1.call-done, bf16[1536,768]{1,0:T(8,128)(2,1)} %all-gather.16.cloned.1.call-done), kind=kOutput, calls=%fused_computation.57 | convolution fusion | flops 3777232896 | bytes 28311552 | tf_op jit(solution)/shard_map/dot_general | solution.py:19
  357.1 9.2 fusion.95
  366.4 138.8 %reduce-scatter.11.cloned.1.call-done = f32[96,768]{1,0:T(8,128)} async-done(((f32[1536,768]{1,0:T(8,128)}), f32[96,768]{1,0:T(8,128)}) %reduce-scatter.11.cloned.1.call-update) | async-done | bytes 294928 | tf_op jit(solution)/shard_map/reduce_scatter | solution.py:192
  505.2 2.5 multiply_reduce_fusion.9
  508.0 62.5 %all-gather.18.cloned.1.call-done = bf16[1536,768]{1,0:T(8,128)(2,1)} async-done(((bf16[96,768]{1,0:T(8,128)(2,1)}), bf16[1536,768]{1,0:T(8,128)(2,1)}) %all-gather.18.cloned.1.call-update) | async-done | bytes 2359312 | tf_op jit(solution)/shard_map/all_gather | solution.py:135
  570.5 8.5 convolution_convert_fusion.1
  579.0 14.0 %add_convert_fusion = bf16[1536,1536]{1,0:T(8,128)(2,1)S(1)} fusion(f32[1536,1536]{1,0:T(8,128)} %get-tuple-element.433, bf16[1536,768]{0,1:T(8,128)(2,1)} %all-gather.22.cloned.1.call-done, bf16[1536,768]{1,0:T(8,128)(2,1)} %all-gather.18.cloned.1.call-done, f32[1536,1536]{1,0:T(8,128)} %get-tuple-element.462), kind=kOutput, calls=%fused_computation.56 | convolution fusion | flops 3656908800 | bytes 28311552 | tf_op jit(solution)/shard_map/dot_general | solution.py:19
  595.2 5.7 fusion.92
  601.5 9.4 fusion.94
  611.6 2.8 broadcast_select_fusion.3
  618.3 3.3 multiply_reduce_fusion.1
  629.6 107.8 %while.29 = (s32[]{:T(128)}, bf16[12,768,64]{1,2,0:T(8,128)(2,1)S(1)}, bf16[12,768,64]{1,2,0:T(8,128)(2,1)}, bf16[12,768,64]{1,2,0:T(8,128)(2,1)}, bf16[12,768,6...) while((s32[]{:T(128)}, ...), condition=%wide.region_17.18_spmd.clone, body=%wide.region_15.17_spmd.clone.sunk | while | flops 383483136 | bytes 19690608 | solution.py:201
  737.4 2.8 fusion.93
  745.7 5.5 fusion.76
  751.2 7.9 reshape.252
  759.1 7.4 fusion.91
  766.6 3.2 copy.140
  769.8 2.4 multiply_reduce_fusion.3
  774.6 2.6 add_add_fusion.2
  779.4 9.9 scatter_custom_fusion
  789.3 5.9 reshape.255
  797.0 2.6 broadcast_select_fusion.1
  799.7 41.4 %all-reduce.5 = f32[3072]{0:T(1024)S(1)} all-reduce(f32[3072]{0:T(1024)S(1)} %pad_maximum_fusion), channel_id=10, replica_groups=mesh['dp'=16,'tensor'=2] {'dp','tensor'}, use_global_device_ids=true, to_apply=%region_45.46.clone | all-reduce | flops 3072 | bytes 24576
  844.6 239.9 %all-reduce.10.cloned.1.call-done = (f32[1769472]{0:T(1024)}, f32[589824]{0:T(1024)}, f32[786432]{0:T(1024)}, f32[1204224]{0:T(1024)}) async-done(((f32[1769472]{0:T(1024)}, f32[589824]{0:T(1024)}, f32[786432]{0:T(1024)}, f32[1204224]{0:T(1024)}), (f32[1769472]{0:T(1024)}, f32[589824]{0:T(1024)}, f32[786432]{0:T(1024)}, f32[1204224]{0:T(1024)})) %all-reduce.10.cloned.1.call-update) | async-done | bytes 17399824
  1084.6 2.7 multiply_reduce_fusion.12
  1087.2 2.5 multiply_reduce_fusion.14
  1094.1 4.5 stack.83
  1098.7 4.6 stack.91
  1104.7 39.6 %all-reduce.6 = (f32[7]{0:T(128)S(1)}, f32[7]{0:T(128)S(1)}) all-reduce(f32[7]{0:T(128)S(1)} %stack.91, f32[7]{0:T(128)S(1)} %stack.83), channel_id=1, replica_groups=mesh['dp'=16,'tensor'=2] {'dp','tensor'}, use_global_device_ids=true, to_apply=%region_47.48 | all-reduce | flops 14 | bytes 112 | tf_op jit(solution)/shard_map/psum | solution.py:250
  (396 shorter events, 244.8 us)
Async XLA Ops:
  7.2 9.9 copy-start.18
  7.2 11.3 copy-start.60
  7.2 54.9 %copy-start.59 = (s32[128]{0:T(128)S(1)}, s32[128]{0:T(128)}, u32[]{:S(2)}) copy-start(s32[128]{0:T(128)} %param.33) | copy-start | bytes 1540
  7.2 54.9 %copy-start.64 = (s32[128]{0:T(128)S(1)}, s32[128]{0:T(128)}, u32[]{:S(2)}) copy-start(s32[128]{0:T(128)} %param.34) | copy-start | bytes 1540
  7.2 61.2 %all-gather.12.cloned.1.call-start = ((), (), s32[]{:S(2)}) async-start(), calls=%async_computation.5 | async-start | bytes 1216512 | tf_op jit(solution)/shard_map/all_gather | solution.py:128
  8.9 126.1 %all-gather.24.cloned.1.call-start = ((), (), s32[]{:S(2)}) async-start(), calls=%async_computation.15 | async-start | bytes 4967424 | tf_op jit(solution)/shard_map/all_gather | solution.py:130
  10.6 186.7 %all-gather.10.cloned.1.call-start = ((), (), s32[]{:S(2)}) async-start(), calls=%async_computation.4 | async-start | bytes 3649536 | tf_op jit(solution)/shard_map/all_gather | solution.py:127
  12.3 292.2 %all-gather.20.cloned.1.call-start = ((), (), s32[]{:S(2)}) async-start(), calls=%async_computation.10 | async-start | bytes 1622016 | tf_op jit(solution)/shard_map/all_gather | solution.py:129
  13.9 305.0 %all-gather.16.cloned.1.call-start = ((), (), s32[]{:S(2)}) async-start(), calls=%async_computation.7 | async-start | bytes 2506752 | tf_op jit(solution)/shard_map/all_gather | solution.py:134
  15.6 314.5 %all-gather.14.cloned.1.call-start = ((), (), s32[]{:S(2)}) async-start(), calls=%async_computation.6 | async-start | bytes 3538944 | tf_op jit(solution)/shard_map/all_gather | solution.py:157
  17.1 187.9 %copy-start.51 = (pred[768]{0:T(1024)(128)(4,1)}, pred[768]{0:T(1024)(128)(4,1)S(1)}, u32[]{:S(2)}) copy-start(pred[768]{0:T(1024)(128)(4,1)S(1)} %compare_and_fusion) | copy-start | bytes 2308
  62.2 142.8 %copy-start.43 = (f32[768]{0:T(1024)}, f32[768]{0:T(1024)S(1)}, u32[]{:S(2)}) copy-start(f32[768]{0:T(1024)S(1)} %get-tuple-element.446) | copy-start | bytes 9220
  62.2 142.8 %copy-start.57 = (f32[768]{0:T(1024)}, f32[768]{0:T(1024)S(1)}, u32[]{:S(2)}) copy-start(f32[768]{0:T(1024)S(1)} %get-tuple-element.447) | copy-start | bytes 9220
  196.3 8.7 copy-start.2
  196.7 8.3 copy-start.36
  197.3 7.7 copy-start.49
  301.3 55.8 %all-gather.22.cloned.1.call-start = ((), (), s32[]{:S(2)}) async-start(), calls=%async_computation.11 | async-start | bytes 3538944 | tf_op jit(solution)/shard_map/all_gather | solution.py:178
  313.4 191.8 %reduce-scatter.11.cloned.1.call-start = ((), (), s32[]{:S(2)}) async-start(), calls=%async_computation.14 | async-start | bytes 5013504 | tf_op jit(solution)/shard_map/reduce_scatter | solution.py:192
  366.3 138.9 %copy-start.22 = (f32[96,768]{1,0:T(8,128)S(1)}, f32[96,768]{1,0:T(8,128)}, u32[]{:S(2)}) copy-start(f32[96,768]{1,0:T(8,128)} %param.49) | copy-start | bytes 884740
  366.3 138.9 %copy-start.32 = (f32[96,768]{1,0:T(8,128)S(1)}, f32[96,768]{1,0:T(8,128)}, u32[]{:S(2)}) copy-start(f32[96,768]{1,0:T(8,128)} %param.51) | copy-start | bytes 884740
  366.3 138.9 %copy-start.33 = (f32[96,768]{1,0:T(8,128)S(1)}, f32[96,768]{1,0:T(8,128)}, u32[]{:S(2)}) copy-start(f32[96,768]{1,0:T(8,128)} %param.50) | copy-start | bytes 884740
  366.4 204.1 %all-gather.18.cloned.1.call-start = ((), (), s32[]{:S(2)}) async-start(), calls=%async_computation.8 | async-start | bytes 2506752 | tf_op jit(solution)/shard_map/all_gather | solution.py:135
  507.8 103.2 %reduce-scatter.5.cloned.1.call-start = ((), (), s32[]{:S(2)}) async-start(), calls=%async_computation.9 | async-start | bytes 3538944 | tf_op jit(solution)/shard_map/reduce_scatter | solution.py:160
  579.0 39.3 %reduce-scatter.7.cloned.1.call-start = ((), (), s32[]{:S(2)}) async-start(), calls=%async_computation.12 | async-start | bytes 7077888 | tf_op jit(solution)/shard_map/reduce_scatter | solution.py:184
  579.0 16.2 %copy-start.67 = (bf16[1536,768]{1,0:T(8,128)(2,1)S(1)}, bf16[1536,768]{1,0:T(8,128)(2,1)}, u32[]{:S(2)}) copy-start(bf16[1536,768]{1,0:T(8,128)(2,1)} %all-gather.16.cloned.1.call-done) | copy-start | bytes 7077892
  601.0 241.4 %reduce-scatter.9.cloned.1.call-start = ((), (), s32[]{:S(2)}) async-start(), calls=%async_computation.13 | async-start | bytes 5013504 | tf_op jit(solution)/shard_map/reduce_scatter | solution.py:191
  610.9 473.7 %all-reduce.10.cloned.1.call-start = ((), (), s32[]{:S(2)}) async-start(), calls=%async_computation.16 | async-start | bytes 34799616
  779.4 9.9 copy-start.13
  797.0 44.2 %copy-start.61 = (f32[96]{0:T(128)S(1)}, f32[96]{0:T(128)}, u32[]{:S(2)}) copy-start(f32[96]{0:T(128)} %param.55) | copy-start | bytes 1156
  797.0 44.2 %copy-start.65 = (f32[96]{0:T(128)S(1)}, f32[96]{0:T(128)}, u32[]{:S(2)}) copy-start(f32[96]{0:T(128)} %param.57) | copy-start | bytes 1156
  797.0 44.1 %copy-start.66 = (f32[96]{0:T(128)S(1)}, f32[96]{0:T(128)}, u32[]{:S(2)}) copy-start(f32[96]{0:T(128)} %param.56) | copy-start | bytes 1156
  797.0 45.4 %copy-start.12 = (f32[96,768]{1,0:T(8,128)S(1)}, f32[96,768]{1,0:T(8,128)}, u32[]{:S(2)}) copy-start(f32[96,768]{1,0:T(8,128)} %param.46) | copy-start | bytes 884740
  797.0 287.6 %copy-start.14 = (f32[55296]{0:T(1024)S(1)}, f32[55296]{0:T(1024)}, u32[]{:S(2)}) copy-start(f32[55296]{0:T(1024)} %param.37) | copy-start | bytes 663556
  799.6 287.6 %copy-start.16 = (f32[37632]{0:T(1024)S(1)}, f32[37632]{0:T(1024)}, u32[]{:S(2)}) copy-start(f32[37632]{0:T(1024)} %param.52) | copy-start | bytes 451588
  799.6 287.6 %copy-start.34 = (f32[37632]{0:T(1024)S(1)}, f32[37632]{0:T(1024)}, u32[]{:S(2)}) copy-start(f32[37632]{0:T(1024)} %param.54) | copy-start | bytes 451588
  799.6 287.6 %copy-start.35 = (f32[37632]{0:T(1024)S(1)}, f32[37632]{0:T(1024)}, u32[]{:S(2)}) copy-start(f32[37632]{0:T(1024)} %param.53) | copy-start | bytes 451588
  799.6 290.1 %copy-start.30 = (f32[24576]{0:T(1024)S(1)}, f32[24576]{0:T(1024)}, u32[]{:S(2)}) copy-start(f32[24576]{0:T(1024)} %param.43) | copy-start | bytes 294916
  799.6 290.1 %copy-start.38 = (f32[24576]{0:T(1024)S(1)}, f32[24576]{0:T(1024)}, u32[]{:S(2)}) copy-start(f32[24576]{0:T(1024)} %param.45) | copy-start | bytes 294916
  799.6 290.1 %copy-start.39 = (f32[24576]{0:T(1024)S(1)}, f32[24576]{0:T(1024)}, u32[]{:S(2)}) copy-start(f32[24576]{0:T(1024)} %param.44) | copy-start | bytes 294916
  799.6 292.3 %copy-start.31 = (f32[18432]{0:T(1024)S(1)}, f32[18432]{0:T(1024)}, u32[]{:S(2)}) copy-start(f32[18432]{0:T(1024)} %param.40) | copy-start | bytes 221188
  799.7 292.3 %copy-start.40 = (f32[18432]{0:T(1024)S(1)}, f32[18432]{0:T(1024)}, u32[]{:S(2)}) copy-start(f32[18432]{0:T(1024)} %param.42) | copy-start | bytes 221188
  799.7 292.3 %copy-start.41 = (f32[18432]{0:T(1024)S(1)}, f32[18432]{0:T(1024)}, u32[]{:S(2)}) copy-start(f32[18432]{0:T(1024)} %param.41) | copy-start | bytes 221188
  842.4 260.9 %copy-start.10 = (bf16[768,768]{0,1:T(8,128)(2,1)S(1)}, bf16[768,768]{0,1:T(8,128)(2,1)}, u32[]{:S(2)}) copy-start(bf16[768,768]{0,1:T(8,128)(2,1)} %get-tuple-element.430) | copy-start | bytes 3538948
  844.6 312.8 %copy-start.28 = (f32[96,768]{1,0:T(8,128)}, f32[96,768]{1,0:T(8,128)S(1)}, u32[]{:S(2)}) copy-start(f32[96,768]{1,0:T(8,128)S(1)} %get-tuple-element.420) | copy-start | bytes 884740
  844.6 312.8 %copy-start.29 = (f32[96,768]{1,0:T(8,128)}, f32[96,768]{1,0:T(8,128)S(1)}, u32[]{:S(2)}) copy-start(f32[96,768]{1,0:T(8,128)S(1)} %get-tuple-element.421) | copy-start | bytes 884740
  1094.1 63.3 %copy-start.23 = (f32[96,768]{1,0:T(8,128)S(1)}, f32[96,768]{1,0:T(8,128)}, u32[]{:S(2)}) copy-start(f32[96,768]{1,0:T(8,128)} %param.49) | copy-start | bytes 884740
  1094.1 63.3 %copy-start.24 = (f32[96,768]{1,0:T(8,128)S(1)}, f32[96,768]{1,0:T(8,128)}, u32[]{:S(2)}) copy-start(f32[96,768]{1,0:T(8,128)} %get-tuple-element.418) | copy-start | bytes 884740
  1094.1 63.3 %copy-start.25 = (f32[96,768]{1,0:T(8,128)S(1)}, f32[96,768]{1,0:T(8,128)}, u32[]{:S(2)}) copy-start(f32[96,768]{1,0:T(8,128)} %get-tuple-element.419) | copy-start | bytes 884740
  (35 other events, 90.0 us)
Sparse Core Ops, SparseCore 0:
  11.6 56.8 all-gather.11
  71.8 63.1 all-gather.23
  138.4 58.8 all-gather.9
  200.6 53.7 all-gather.19
  257.7 61.1 all-gather.15
  320.3 9.7 all-gather.13
  331.6 12.1 all-gather.21
  366.5 138.6 reduce-scatter.10
  508.9 61.4 all-gather.17
  579.1 8.7 reduce-scatter.4
  601.1 11.3 reduce-scatter.6
  618.4 138.7 reduce-scatter.8
  795.4 289.1 all-reduce.9
where the time goes:
time: 1180 us; the launch traced here: 1170 us
  waiting for transfers between devices  526 us (45%)
  matrix products  248 us (21%)
  other arithmetic  125 us (11%)
  blocking collectives  123 us (10%)
  local copies, waits for them, and re-layouts  122 us (10%)
  between operations  19.4 us (2%)
    unnamed x14, waiting for transfers between devices  240 us
    dot_general x70, matrix products, contract(): lax.dot_general(left, right, (((left_dim,), (right_dim,)), ((), ())), pre...  180 us
    reduce_scatter x1, waiting for transfers between devices, local(): lax.psum_scatter(grad_reduce, 'dp', scatter_dimension=0, tiled=True)  139 us
    unnamed x2, blocking collectives  83.7 us
    all_gather x1, waiting for transfers between devices, local(): lax.all_gather(position_table.astype(jnp.bfloat16), ('dp', 'tensor'), axi...  63.2 us
    all_gather x1, waiting for transfers between devices, local(): lax.all_gather(reduce_weight.astype(jnp.bfloat16), 'dp', axis=0, tiled=True)  62.5 us
    all_gather x1, other arithmetic, local(): lax.all_gather(position_table.astype(jnp.bfloat16), ('dp', 'tensor'), axi...  51.2 us
    psum x1, blocking collectives, local(): lax.psum((jnp.stack([jnp.sum(master * master) for master in masters]), up...  39.6 us
  transfers between devices with their start and end apart: 13, of which 7 were waited for; matrix products, arithmetic and copies ran while one was open for 37% of the time, Pallas kernels for 0%

commit v1 on v0

--- a/solution.py
+++ b/solution.py
@@ -13,6 +13,16 @@
 ADAM_EPS = 1e-06
 DECAY = 0.05
 TINY = 1e-06
+
+
+def collect(x, axis, dim):
+    ways, here, step = (lax.axis_size(axis), lax.axis_index(axis), x.shape[dim])
+    dims = [n * ways if d == dim else n for d, n in enumerate(x.shape)]
+    full = lax.dynamic_update_slice_in_dim(jnp.zeros(dims, x.dtype), x, here * step, axis=dim)
+    for far in range(1, ways):
+        x = lax.ppermute(x, axis, [(d, (d + 1) % ways) for d in range(ways)])
+        full = lax.dynamic_update_slice_in_dim(full, x, (here - far) % ways * step, axis=dim)
+    return full
 
 
 def contract(left, right, left_dim, right_dim):
@@ -132,7 +142,7 @@
     )
     expand_low, reduce_low = (
         lax.all_gather(expand_weight.astype(jnp.bfloat16), "dp", axis=0, tiled=True),
-        lax.all_gather(reduce_weight.astype(jnp.bfloat16), "dp", axis=0, tiled=True),
+        collect(reduce_weight.astype(jnp.bfloat16), "dp", 0),
     )
     entry_low = gathered[0].reshape(model_width, 3 * model_width)
     exit_low = gathered[1].reshape(model_width, model_width)

time: 1180 us -> 1130 us (0.958)
  waiting for transfers between devices: 526 us -> 465 us
  local copies, waits for them, and re-layouts: 122 us -> 144 us
    ppermute x0 -> x15, waiting for transfers between devices: none -> 99.6 us  [collect(): x = lax.ppermute(x, axis, [(d, (d + 1) % ways) for d in range(ways)])]
    reduce_scatter x1, waiting for transfers between devices: 139 us -> 46.9 us  [local(): lax.psum_scatter(grad_reduce, 'dp', scatter_dimension=0, tiled=True)]
    all_gather x1 -> x0, waiting for transfers between devices: 62.5 us -> none  [local(): lax.all_gather(reduce_weight.astype(jnp.bfloat16), 'dp', axis=0, tiled=True)]
    unnamed x14 -> x13, waiting for transfers between devices: 240 us -> 293 us
    all_gather x1, waiting for transfers between devices: 63.2 us -> 25.6 us  [local(): lax.all_gather(position_table.astype(jnp.bfloat16), ('dp', 'tensor'), axi...]
    dynamic_update_slice x0 -> x15, local copies, waits for them, and re-layouts: none -> 17.3 us  [collect(): lax.dynamic_update_slice_in_dim(full, x, (here - far) % ways * step, axis...]
    unnamed x151 -> x159, local copies, waits for them, and re-layouts: 29.1 us -> 32.4 us
  transfers between devices with their start and end apart: 13 -> 27, of which waited for: 7 -> 16; matrix products, arithmetic and copies ran while one was open for 37% -> 42% of each run, Pallas kernels for 0% -> 0%
where the time goes in v1:
time: 1130 us; the launch traced here: 1120 us
  waiting for transfers between devices  465 us (41%)
  matrix products  246 us (22%)
  local copies, waits for them, and re-layouts  144 us (13%)
  other arithmetic  122 us (11%)
  blocking collectives  117 us (10%)
  between operations  19.8 us (2%)
    unnamed x13, waiting for transfers between devices  293 us
    dot_general x70, matrix products, contract(): lax.dot_general(left, right, (((left_dim,), (right_dim,)), ((), ())), pre...  181 us
    ppermute x15, waiting for transfers between devices, collect(): x = lax.ppermute(x, axis, [(d, (d + 1) % ways) for d in range(ways)])  99.6 us
    unnamed x2, blocking collectives  77.8 us
    all_gather x1, other arithmetic, local(): lax.all_gather(position_table.astype(jnp.bfloat16), ('dp', 'tensor'), axi...  51.2 us
    reduce_scatter x1, waiting for transfers between devices, local(): lax.psum_scatter(grad_reduce, 'dp', scatter_dimension=0, tiled=True)  46.9 us
    psum x1, blocking collectives, local(): lax.psum((jnp.stack([jnp.sum(master * master) for master in masters]), up...  39.6 us
    unnamed x159, local copies, waits for them, and re-layouts  32.4 us
  transfers between devices with their start and end apart: 27, of which 16 were waited for; matrix products, arithmetic and copies ran while one was open for 42% of the time, Pallas kernels for 0%

profile of v1, /device:TPU:0, one launch (start us, length us, event | category | flops | bytes accessed | tf_op | source)
XLA Modules:
  0.0 1122.5 jit_solution(6927053213004350754)
XLA Ops:
  21.3 40.6 %all-reduce = bf16[3072]{0:T(1024)(128)(2,1)S(1)} all-reduce(bf16[3072]{0:T(1024)(128)(2,1)S(1)} %dynamic-update-slice), channel_id=1, replica_groups=mesh['dp'=16,'tensor'=2] {'dp','tensor'}, use_global_device_ids=true, to_apply=%add | all-reduce | flops 3072 | bytes 12288
  64.8 6.6 collective-permute-done.1
  71.4 8.7 collective-permute-done.2
  80.3 9.3 collective-permute-done.3
  90.2 8.0 collective-permute-done.4
  99.8 8.4 collective-permute-done.5
  108.6 3.3 reshape.249
  111.9 25.6 %all-gather.21.cloned.1.call-done = bf16[32,1,37632]{2,1,0:T(2,128)(2,1)} async-done(((bf16[1,1,37632]{2,1,0:T(2,128)(2,1)}), bf16[32,1,37632]{2,1,0:T(2,128)(2,1)}) %all-gather.21.cloned.1.call-update) | async-done | bytes 2408464 | tf_op jit(solution)/shard_map/all_gather | solution.py:140
  137.5 51.2 %reduce.1 = bf16[32,37632]{1,0:T(8,128)(2,1)} reduce(bf16[32,1,37632]{2,1,0:T(2,128)(2,1)} %all-gather.21.cloned.1.call-done, bf16[]{:T(256)} %constant.343), dimensions={1}, to_apply=%all-gather.reduce_sub_computation | reduce | bytes 4816898 | tf_op jit(solution)/shard_map/all_gather | solution.py:140
  188.7 5.0 reshape.244
  193.7 3.4 gather_fusion
  199.9 7.6 reshape.245
  207.6 6.7 convolution_convert_fusion
  214.3 6.3 copy.127
  220.6 3.3 slice_bitcast_fusion
  223.8 3.7 copy.129
  233.5 64.8 %while.28 = (s32[]{:T(128)}, bf16[12,768,64]{1,2,0:T(8,128)(2,1)}, f32[12,768]{1,0:T(8,128)}, bf16[12,768,64]{2,1,0:T(8,128)(2,1)}, bf16[12,768,64]{2,1,0:T(8,12...) while((s32[]{:T(128)}, bf16[12,768,64]{1,2,0:T(8,128)(2,1)}, ...), condition=%wide.region_8.9_spmd.clone, body=%wide.region_5.8_spmd.clone.sunk | while | flops 156302592 | bytes 7911521 | solution.py:160
  298.3 3.2 fusion.89
  308.1 9.5 collective-permute-done.7
  320.7 9.2 collective-permute-done.8
  333.1 5.6 collective-permute-done.9
  341.9 5.6 collective-permute-done.10
  350.6 5.6 collective-permute-done.11
  357.5 7.4 collective-permute-done.12
  366.3 8.3 collective-permute-done.13
  375.9 7.4 collective-permute-done.14
  384.0 3.7 reshape.250
  387.7 5.2 fusion.90
  393.0 27.8 %multiply_convert_fusion.1 = (bf16[1536,1536]{1,0:T(8,128)(2,1)S(1)}, f32[1536,1536]{1,0:T(8,128)}, f32[1536,1536]{1,0:T(8,128)}) fusion(bf16[1536,768]{0,1:T(8,128)(2,1)} %all-gather.13.cloned.1.call-done, bf16[1536,768]{1,0:T(8,128)(2,1)} %all-gather.15.cloned.1.call-done), kind=kOutput, calls=%fused_computation.57 | convolution fusion | flops 3777232896 | bytes 28311552 | tf_op jit(solution)/shard_map/dot_general | solution.py:29
  423.0 5.4 convolution_convert_fusion.1
  428.5 14.6 %add_convert_fusion = bf16[1536,1536]{1,0:T(8,128)(2,1)S(1)} fusion(f32[1536,1536]{1,0:T(8,128)} %get-tuple-element.435, bf16[1536,768]{0,1:T(8,128)(2,1)} %all-gather.19.cloned.1.call-done, bf16[1536,768]{1,0:T(8,128)(2,1)} %constant_dynamic-update-slice_fusion, f32[1536,1536]{1,0:T(8,128)} %get-tuple-element.463), kind=kOutput, calls=%fused_computation.56 | convolution fusion | flops 3656908800 | bytes 28311552 | tf_op jit(solution)/shard_map/dot_general | solution.py:29
  445.3 5.7 fusion.92
  451.1 10.0 fusion.94
  461.5 9.1 fusion.95
  478.0 3.3 multiply_reduce_fusion.1
  489.4 107.5 %while.29 = (s32[]{:T(128)}, bf16[12,768,64]{1,2,0:T(8,128)(2,1)S(1)}, bf16[12,768,64]{1,2,0:T(8,128)(2,1)}, bf16[12,768,64]{1,2,0:T(8,128)(2,1)}, bf16[12,768,6...) while((s32[]{:T(128)}, ...), condition=%wide.region_17.18_spmd.clone, body=%wide.region_15.17_spmd.clone.sunk | while | flops 383483136 | bytes 19690608 | solution.py:211
  605.1 5.5 fusion.76
  610.6 7.9 reshape.252
  618.5 7.4 fusion.91
  626.0 3.1 copy.140
  638.8 9.8 scatter_custom_fusion
  648.7 6.0 reshape.255
  659.0 37.1 %all-reduce.5 = f32[3072]{0:T(1024)S(1)} all-reduce(f32[3072]{0:T(1024)S(1)} %pad_maximum_fusion), channel_id=10, replica_groups=mesh['dp'=16,'tensor'=2] {'dp','tensor'}, use_global_device_ids=true, to_apply=%region_45.46.clone | all-reduce | flops 3072 | bytes 24576
  699.4 46.9 %reduce-scatter.11.cloned.1.call-done = f32[96,768]{1,0:T(8,128)} async-done(((f32[1536,768]{1,0:T(8,128)}), f32[96,768]{1,0:T(8,128)}) %reduce-scatter.11.cloned.1.call-update) | async-done | bytes 294928 | tf_op jit(solution)/shard_map/reduce_scatter | solution.py:202
  748.3 292.7 %all-reduce.10.cloned.1.call-done = (f32[1769472]{0:T(1024)}, f32[589824]{0:T(1024)}, f32[786432]{0:T(1024)}, f32[1204224]{0:T(1024)}) async-done(((f32[1769472]{0:T(1024)}, f32[589824]{0:T(1024)}, f32[786432]{0:T(1024)}, f32[1204224]{0:T(1024)}), (f32[1769472]{0:T(1024)}, f32[589824]{0:T(1024)}, f32[786432]{0:T(1024)}, f32[1204224]{0:T(1024)})) %all-reduce.10.cloned.1.call-update) | async-done | bytes 17399824
  1050.9 4.6 stack.83
  1055.6 4.6 stack.91
  1061.6 39.6 %all-reduce.6 = (f32[7]{0:T(128)S(1)}, f32[7]{0:T(128)S(1)}) all-reduce(f32[7]{0:T(128)S(1)} %stack.91, f32[7]{0:T(128)S(1)} %stack.83), channel_id=1, replica_groups=mesh['dp'=16,'tensor'=2] {'dp','tensor'}, use_global_device_ids=true, to_apply=%region_47.48 | all-reduce | flops 14 | bytes 112 | tf_op jit(solution)/shard_map/psum | solution.py:260
  (448 shorter events, 292.6 us)
Async XLA Ops:
  7.2 101.3 %all-gather.11.cloned.1.call-start = ((), (), s32[]{:S(2)}) async-start(), calls=%async_computation.5 | async-start | bytes 1216512 | tf_op jit(solution)/shard_map/all_gather | solution.py:138
  8.9 128.6 %all-gather.21.cloned.1.call-start = ((), (), s32[]{:S(2)}) async-start(), calls=%async_computation.14 | async-start | bytes 4967424 | tf_op jit(solution)/shard_map/all_gather | solution.py:140
  10.6 60.8 %copy-start.59 = (s32[768]{0:T(1024)S(1)}, s32[768]{0:T(1024)}, u32[]{:S(2)}) copy-start(s32[768]{0:T(1024)} %param.32) | copy-start | bytes 9220
  10.6 87.7 %copy-start.23 = (bf16[768,768]{1,0:T(8,128)(2,1)S(1)}, bf16[768,768]{1,0:T(8,128)(2,1)}, u32[]{:S(2)}) copy-start(bf16[768,768]{1,0:T(8,128)(2,1)} %param.31) | copy-start | bytes 3538948
  10.6 189.3 %all-gather.9.cloned.1.call-start = ((), (), s32[]{:S(2)}) async-start(), calls=%async_computation.4 | async-start | bytes 3649536 | tf_op jit(solution)/shard_map/all_gather | solution.py:137
  12.4 371.6 %all-gather.17.cloned.1.call-start = ((), (), s32[]{:S(2)}) async-start(), calls=%async_computation.9 | async-start | bytes 1622016 | tf_op jit(solution)/shard_map/all_gather | solution.py:139
  14.0 379.0 %all-gather.15.cloned.1.call-start = ((), (), s32[]{:S(2)}) async-start(), calls=%async_computation.7 | async-start | bytes 2506752 | tf_op jit(solution)/shard_map/all_gather | solution.py:144
  15.6 46.3 %collective-permute-start = (bf16[96,768]{1,0:T(8,128)(2,1)S(1)}, bf16[96,768]{1,0:T(8,128)(2,1)S(1)}, u32[]{:S(2)}, u32[]{:S(2)}) collective-permute-start(bf16[96,768]{1,0:T(8,128)(2,1)S(1)} %get-tuple-element.433), channel_id=1, source_target_pairs={{0,2},{2,4},{4,6},{6,8},{8,10},{10,12},{12,14},{14,16},{16,18},{18... | collective-permute-start | bytes 442376 | tf_op jit(solution)/shard_map/ppermute | solution.py:23
  19.3 373.7 %all-gather.13.cloned.1.call-start = ((), (), s32[]{:S(2)}) async-start(), calls=%async_computation.6 | async-start | bytes 3538944 | tf_op jit(solution)/shard_map/all_gather | solution.py:167
  61.9 50.0 %copy-start.35 = (bf16[96,768]{1,0:T(8,128)(2,1)}, bf16[96,768]{1,0:T(8,128)(2,1)S(1)}, u32[]{:S(2)}) copy-start(bf16[96,768]{1,0:T(8,128)(2,1)S(1)} %collective-permute-done) | copy-start | bytes 442372
  61.9 9.4 collective-permute-start.1
  64.8 142.7 %copy-start.45 = (f32[768]{0:T(1024)}, f32[768]{0:T(1024)S(1)}, u32[]{:S(2)}) copy-start(f32[768]{0:T(1024)S(1)} %get-tuple-element.447) | copy-start | bytes 9220
  64.8 142.7 %copy-start.60 = (f32[768]{0:T(1024)}, f32[768]{0:T(1024)S(1)}, u32[]{:S(2)}) copy-start(f32[768]{0:T(1024)S(1)} %get-tuple-element.448) | copy-start | bytes 9220
  71.3 40.6 %copy-start.36 = (bf16[96,768]{1,0:T(8,128)(2,1)}, bf16[96,768]{1,0:T(8,128)(2,1)S(1)}, u32[]{:S(2)}) copy-start(bf16[96,768]{1,0:T(8,128)(2,1)S(1)} %collective-permute-done.1) | copy-start | bytes 442372
  71.3 8.7 collective-permute-start.2
  80.1 9.5 collective-permute-start.3
  89.5 8.7 collective-permute-start.4
  98.3 10.0 collective-permute-start.5
  98.3 109.2 %copy-start.53 = (pred[768]{0:T(1024)(128)(4,1)}, pred[768]{0:T(1024)(128)(4,1)S(1)}, u32[]{:S(2)}) copy-start(pred[768]{0:T(1024)(128)(4,1)S(1)} %compare_and_fusion) | copy-start | bytes 2308
  108.2 195.8 %collective-permute-start.6 = (bf16[96,768]{1,0:T(8,128)(2,1)}, bf16[96,768]{1,0:T(8,128)(2,1)}, u32[]{:S(2)}, u32[]{:S(2)}) collective-permute-start(bf16[96,768]{1,0:T(8,128)(2,1)} %collective-permute-done.5), channel_id=1, source_target_pairs={{0,2},{2,4},{4,6},{6,8},{8,10},{10,12},{12,14},{14,16},{16,18},{18... | collective-permute-start | bytes 442376 | tf_op jit(solution)/shard_map/ppermute | solution.py:23
  303.9 124.5 %all-gather.19.cloned.1.call-start = ((), (), s32[]{:S(2)}) async-start(), calls=%async_computation.10 | async-start | bytes 3538944 | tf_op jit(solution)/shard_map/all_gather | solution.py:188
  304.0 13.6 %collective-permute-start.7 = (bf16[96,768]{1,0:T(8,128)(2,1)}, bf16[96,768]{1,0:T(8,128)(2,1)}, u32[]{:S(2)}, u32[]{:S(2)}) collective-permute-start(bf16[96,768]{1,0:T(8,128)(2,1)} %collective-permute-done.6), channel_id=1, source_target_pairs={{0,2},{2,4},{4,6},{6,8},{8,10},{10,12},{12,14},{14,16},{16,18},{18... | collective-permute-start | bytes 442376 | tf_op jit(solution)/shard_map/ppermute | solution.py:23
  317.6 12.4 %collective-permute-start.8 = (bf16[96,768]{1,0:T(8,128)(2,1)}, bf16[96,768]{1,0:T(8,128)(2,1)S(1)}, u32[]{:S(2)}, u32[]{:S(2)}) collective-permute-start(bf16[96,768]{1,0:T(8,128)(2,1)} %collective-permute-done.7), channel_id=1, source_target_pairs={{0,2},{2,4},{4,6},{6,8},{8,10},{10,12},{12,14},{14,16},{16,18},{18... | collective-permute-start | bytes 442376 | tf_op jit(solution)/shard_map/ppermute | solution.py:23
  330.0 8.7 collective-permute-start.9
  338.7 8.7 collective-permute-start.10
  347.4 8.7 collective-permute-start.11
  356.2 8.7 collective-permute-start.12
  364.9 9.7 collective-permute-start.13
  374.6 8.7 collective-permute-start.14
  392.9 77.8 %reduce-scatter.5.cloned.1.call-start = ((), (), s32[]{:S(2)}) async-start(), calls=%async_computation.8 | async-start | bytes 3538944 | tf_op jit(solution)/shard_map/reduce_scatter | solution.py:170
  428.4 49.6 %reduce-scatter.7.cloned.1.call-start = ((), (), s32[]{:S(2)}) async-start(), calls=%async_computation.11 | async-start | bytes 7077888 | tf_op jit(solution)/shard_map/reduce_scatter | solution.py:194
  451.0 246.4 %reduce-scatter.9.cloned.1.call-start = ((), (), s32[]{:S(2)}) async-start(), calls=%async_computation.12 | async-start | bytes 5013504 | tf_op jit(solution)/shard_map/reduce_scatter | solution.py:201
  461.0 285.3 %reduce-scatter.11.cloned.1.call-start = ((), (), s32[]{:S(2)}) async-start(), calls=%async_computation.13 | async-start | bytes 5013504 | tf_op jit(solution)/shard_map/reduce_scatter | solution.py:202
  470.6 570.5 %all-reduce.10.cloned.1.call-start = ((), (), s32[]{:S(2)}) async-start(), calls=%async_computation.15 | async-start | bytes 34799616
  656.4 39.8 %copy-start.64 = (f32[96]{0:T(128)S(1)}, f32[96]{0:T(128)}, u32[]{:S(2)}) copy-start(f32[96]{0:T(128)} %param.55) | copy-start | bytes 1156
  656.4 39.8 %copy-start.68 = (f32[96]{0:T(128)S(1)}, f32[96]{0:T(128)}, u32[]{:S(2)}) copy-start(f32[96]{0:T(128)} %param.57) | copy-start | bytes 1156
  656.4 39.7 %copy-start.69 = (f32[96]{0:T(128)S(1)}, f32[96]{0:T(128)}, u32[]{:S(2)}) copy-start(f32[96]{0:T(128)} %param.56) | copy-start | bytes 1156
  656.4 41.0 %copy-start.13 = (f32[96,768]{1,0:T(8,128)S(1)}, f32[96,768]{1,0:T(8,128)}, u32[]{:S(2)}) copy-start(f32[96,768]{1,0:T(8,128)} %param.46) | copy-start | bytes 884740
  656.4 89.9 %copy-start.15 = (f32[96,768]{1,0:T(8,128)S(1)}, f32[96,768]{1,0:T(8,128)}, u32[]{:S(2)}) copy-start(f32[96,768]{1,0:T(8,128)} %param.49) | copy-start | bytes 884740
  659.0 382.1 %copy-start.19 = (f32[55296]{0:T(1024)S(1)}, f32[55296]{0:T(1024)}, u32[]{:S(2)}) copy-start(f32[55296]{0:T(1024)} %param.37) | copy-start | bytes 663556
  697.4 346.4 %copy-start.21 = (f32[37632]{0:T(1024)S(1)}, f32[37632]{0:T(1024)}, u32[]{:S(2)}) copy-start(f32[37632]{0:T(1024)} %param.52) | copy-start | bytes 451588
  699.4 414.9 %copy-start.29 = (f32[96,768]{1,0:T(8,128)}, f32[96,768]{1,0:T(8,128)S(1)}, u32[]{:S(2)}) copy-start(f32[96,768]{1,0:T(8,128)S(1)} %get-tuple-element.420) | copy-start | bytes 884740
  699.4 414.9 %copy-start.30 = (f32[96,768]{1,0:T(8,128)}, f32[96,768]{1,0:T(8,128)S(1)}, u32[]{:S(2)}) copy-start(f32[96,768]{1,0:T(8,128)S(1)} %get-tuple-element.421) | copy-start | bytes 884740
  699.4 347.0 %copy-start.33 = (f32[24576]{0:T(1024)S(1)}, f32[24576]{0:T(1024)}, u32[]{:S(2)}) copy-start(f32[24576]{0:T(1024)} %param.43) | copy-start | bytes 294916
  699.4 349.3 %copy-start.34 = (f32[18432]{0:T(1024)S(1)}, f32[18432]{0:T(1024)}, u32[]{:S(2)}) copy-start(f32[18432]{0:T(1024)} %param.40) | copy-start | bytes 221188
  699.4 360.7 %copy-start.10 = (bf16[768,768]{0,1:T(8,128)(2,1)S(1)}, bf16[768,768]{0,1:T(8,128)(2,1)}, u32[]{:S(2)}) copy-start(bf16[768,768]{0,1:T(8,128)(2,1)} %get-tuple-element.430) | copy-start | bytes 3538948
  748.3 365.9 %copy-start.31 = (f32[96,768]{1,0:T(8,128)}, f32[96,768]{1,0:T(8,128)S(1)}, u32[]{:S(2)}) copy-start(f32[96,768]{1,0:T(8,128)S(1)} %get-tuple-element.418) | copy-start | bytes 884740
  748.3 365.9 %copy-start.32 = (f32[96,768]{1,0:T(8,128)}, f32[96,768]{1,0:T(8,128)S(1)}, u32[]{:S(2)}) copy-start(f32[96,768]{1,0:T(8,128)S(1)} %get-tuple-element.419) | copy-start | bytes 884740
  (53 other events, 310.0 us)
Sparse Core Ops, SparseCore 0:
  11.5 56.9 all-gather.10
  71.9 65.6 all-gather.20
  141.0 58.8 all-gather.8
  203.2 53.7 all-gather.16
  260.2 64.4 all-gather.14
  326.2 13.5 all-gather.12
  393.1 6.8 all-gather.18
  428.5 5.7 reduce-scatter.4
  451.1 8.4 reduce-scatter.6
  464.7 138.8 reduce-scatter.8
  609.5 136.7 reduce-scatter.10
  752.6 288.4 all-reduce.9
